TPU v7x, 32 devices: a whole 2x2x4 slice. The times are simulated.
32 devices in a mesh: shard: 8 (over z, x), rep: 4 (over y, core).
Axes of the slice: x: 2, y: 2, z: 4, core: 2. Of those that a mesh axis runs over, the one named last changes fastest.
Arguments:
- images: bfloat16 [32, 197, 768], P(('shard', 'rep')), may hold values from -6 to 6
- cotangent: bfloat16 [32, 197, 768], P(('shard', 'rep')), may hold values from -6 to 6
- weights_in: float32 [768, 6144], P('shard'), may hold values from -13 to 13
- weights_down: float32 [3072, 768], P('shard'), may hold values from -0.109375 to 0.109375
- vectors: float32 [12, 768], P(None, 'shard'), may hold values from -1.5 to 1.5, as said below
- mean_in: float32 [768, 6144], P('shard'), may hold values from -256 to 256
- mean_down: float32 [3072, 768], P('shard'), may hold values from -256 to 256
- mean_vectors: float32 [12, 768], P(None, 'shard'), may hold values from -256 to 256
- square_in: float32 [768, 6144], P('shard'), may hold values from 63.04 to 6304
- square_down: float32 [3072, 768], P('shard'), may hold values from 63.04 to 6304
- square_vectors: float32 [12, 768], P(None, 'shard'), may hold values from 63.04 to 6304
Outputs:
- block_out: bfloat16 [32, 197, 768], P(('shard', 'rep'))
- input_grad: float32 [32, 197, 768], P(('shard', 'rep'))
- grad_in: float32 [768, 6144], P('shard')
- grad_down: float32 [3072, 768], P('shard')
- grad_vectors: float32 [12, 768], P(None, 'shard')
- updated_in: float32 [768, 6144], P('shard')
- updated_down: float32 [3072, 768], P('shard')
- updated_vectors: float32 [12, 768], P(None, 'shard')
- next_mean_in: float32 [768, 6144], P('shard')
- next_mean_down: float32 [3072, 768], P('shard')
- next_mean_vectors: float32 [12, 768], P(None, 'shard')
- next_square_in: float32 [768, 6144], P('shard')
- next_square_down: float32 [3072, 768], P('shard')
- next_square_vectors: float32 [12, 768], P(None, 'shard')
Inputs may be any that keep to these rules, and one draw needn't show every extreme that they name: `vectors`: rows 0 and 5 are the norms' gains.
All inputs are finite; a program needn't handle non-finite values.
Results may differ from a plain program's by a relative error of at most 0.023.
Values may be sent and summed in bfloat16 or wider, within the bound.
A program may use at most 128 MiB of HBM per device.

v0:
```python
import math
import jax
import jax.numpy as jnp
from jax import lax
from jax.sharding import PartitionSpec as P

HEADS = 12
NORM_EPS = 1e-06
BETA_ONE = 0.9
BETA_TWO = 0.95
ADAM_EPS = 1e-08
RATE_MATRIX = 0.008
RATE_VECTOR = 0.15
DECAY_MATRIX = 0.05
STEP_COUNT = 2.0


def to_half(array_in):
    return array_in.astype(jnp.bfloat16)


def matmul(left, right):
    return jnp.dot(left, right, preferred_element_type=jnp.float32)


def times_transposed(left, right):
    return lax.dot_general(
        left, right, (((1,), (1,)), ((), ())), preferred_element_type=jnp.float32
    )


def transposed_times(left, right):
    return lax.dot_general(
        left, right, (((0,), (0,)), ((), ())), preferred_element_type=jnp.float32
    )


def layer_norm(inputs, gain, shift):
    centred = inputs - jnp.mean(inputs, axis=-1, keepdims=True)
    inv_std = lax.rsqrt(jnp.mean(centred * centred, axis=-1, keepdims=True) + NORM_EPS)
    normed = centred * inv_std
    return (normed, inv_std, normed * gain + shift)


def norm_back(grad_after, normed, inv_std, gain):
    grad_normed = grad_after * gain
    grad_inputs = inv_std * (
        grad_normed
        - jnp.mean(grad_normed, axis=-1, keepdims=True)
        - normed * jnp.mean(grad_normed * normed, axis=-1, keepdims=True)
    )
    return (grad_inputs, jnp.sum(grad_after * normed, axis=0), jnp.sum(grad_after, axis=0))


def gaussian_unit(hidden):
    cdf_part = 0.5 * (1.0 + jax.scipy.special.erf(hidden * 0.7071067811865476))
    slope = cdf_part + hidden * jnp.exp(-0.5 * hidden * hidden) * 0.3989422804014327
    return (hidden * cdf_part, slope)


def head_scores(query_heads, key_heads, score_scale):
    return (
        jnp.einsum("bqhe,bkhe->bhqk", query_heads, key_heads, preferred_element_type=jnp.float32)
        * score_scale
    )


def forward_pass(images, matrix_half, down_half, vector_half):
    img_count, seq_len, model_width = images.shape
    head_dim = model_width // HEADS
    score_scale = 1.0 / math.sqrt(head_dim)
    row_count = img_count * seq_len
    head_shape = (img_count, seq_len, HEADS, head_dim)
    vector_float = vector_half.astype(jnp.float32)
    flat_in = images.reshape(row_count, model_width).astype(jnp.float32)
    normed_one, inv_one, pre_one = layer_norm(flat_in, vector_float[0], vector_float[1])
    act_one = to_half(pre_one)
    projected = matmul(act_one, matrix_half[:, : 3 * model_width])
    query_heads = to_half(projected[:, :model_width] + vector_float[2]).reshape(head_shape)
    key_heads = to_half(projected[:, model_width : 2 * model_width]).reshape(head_shape)
    value_heads = to_half(projected[:, 2 * model_width :] + vector_float[3]).reshape(head_shape)
    scores = head_scores(query_heads, key_heads, score_scale)
    log_total = jax.nn.logsumexp(scores, axis=-1, keepdims=True)
    probs_half = to_half(jnp.exp(scores - log_total))
    attended = to_half(
        jnp.einsum(
            "bhqk,bkhe->bqhe", probs_half, value_heads, preferred_element_type=jnp.float32
        ).reshape(row_count, model_width)
    )
    hidden_one = (
        flat_in
        + matmul(attended, matrix_half[:, 3 * model_width : 4 * model_width])
        + vector_float[4]
    )
    normed_two, inv_two, pre_two = layer_norm(hidden_one, vector_float[5], vector_float[6])
    act_two = to_half(pre_two)
    up_input = matmul(act_two, matrix_half[:, 4 * model_width :]) + vector_float[8:].reshape(-1)
    gelu_out, gelu_slope = gaussian_unit(up_input)
    gelu_half = to_half(gelu_out)
    block_out = to_half(hidden_one + matmul(gelu_half, down_half) + vector_float[7])
    saved = (
        normed_one,
        inv_one,
        act_one,
        query_heads,
        key_heads,
        value_heads,
        log_total,
        attended,
        normed_two,
        inv_two,
        act_two,
        gelu_slope,
        gelu_half,
    )
    return (block_out.reshape(images.shape), saved)


def backward_pass(cotangent, saved, matrix_half, down_half, vector_half):
    (
        normed_one,
        inv_one,
        act_one,
        query_heads,
        key_heads,
        value_heads,
        log_total,
        attended,
        normed_two,
        inv_two,
        act_two,
        gelu_slope,
        gelu_half,
    ) = saved
    img_count, seq_len, model_width = cotangent.shape
    head_dim = model_width // HEADS
    score_scale = 1.0 / math.sqrt(head_dim)
    row_count = img_count * seq_len
    head_shape = (img_count, seq_len, HEADS, head_dim)
    vector_float = vector_half.astype(jnp.float32)
    joint_weights = matrix_half[:, : 3 * model_width]
    output_weights = matrix_half[:, 3 * model_width : 4 * model_width]
    upward_weights = matrix_half[:, 4 * model_width :]
    grad_half = cotangent.reshape(row_count, model_width)
    grad_out = grad_half.astype(jnp.float32)
    grad_up = times_transposed(grad_half, down_half) * gelu_slope
    up_half = to_half(grad_up)
    grad_act_two = times_transposed(up_half, upward_weights)
    grad_norm_two, grad_gain_two, grad_shift_two = norm_back(
        grad_act_two, normed_two, inv_two, vector_float[5]
    )
    grad_hidden = grad_out + grad_norm_two
    hidden_half = to_half(grad_hidden)
    grad_att = to_half(times_transposed(hidden_half, output_weights)).reshape(head_shape)
    prob_float = jnp.exp(head_scores(query_heads, key_heads, score_scale) - log_total)
    probs_half = to_half(prob_float)
    grad_probs = jnp.einsum(
        "bqhe,bkhe->bhqk", grad_att, value_heads, preferred_element_type=jnp.float32
    )
    row_inner = jnp.sum(prob_float * grad_probs, axis=-1, keepdims=True)
    grad_scores = to_half(prob_float * (grad_probs - row_inner) * score_scale)
    grad_query = jnp.einsum(
        "bhqk,bkhe->bqhe", grad_scores, key_heads, preferred_element_type=jnp.float32
    ).reshape(row_count, model_width)
    grad_key = jnp.einsum(
        "bhqk,bqhe->bkhe", grad_scores, query_heads, preferred_element_type=jnp.float32
    ).reshape(row_count, model_width)
    grad_value = jnp.einsum(
        "bhqk,bqhe->bkhe", probs_half, grad_att, preferred_element_type=jnp.float32
    ).reshape(row_count, model_width)
    grad_proj = to_half(jnp.concatenate([grad_query, grad_key, grad_value], axis=1))
    grad_act_one = times_transposed(grad_proj, joint_weights)
    grad_norm_one, grad_gain_one, grad_shift_one = norm_back(
        grad_act_one, normed_one, inv_one, vector_float[0]
    )
    input_grad = (grad_hidden + grad_norm_one).reshape(cotangent.shape)
    grad_down = transposed_times(gelu_half, grad_half)
    small_rows = jnp.stack(
        [
            grad_gain_one,
            grad_shift_one,
            jnp.sum(grad_query, axis=0),
            jnp.sum(grad_value, axis=0),
            jnp.sum(grad_hidden, axis=0),
            grad_gain_two,
            grad_shift_two,
            jnp.sum(grad_out, axis=0),
        ]
    )
    grad_vectors = jnp.concatenate(
        [small_rows, jnp.sum(grad_up, axis=0).reshape(4, model_width)], axis=0
    )
    factors = (act_one, grad_proj, attended, hidden_half, act_two, up_half)
    return (input_grad, grad_down, grad_vectors, factors)


def adam_update(weights, first, second, gradient, rate, decay):
    next_first = BETA_ONE * first + (1.0 - BETA_ONE) * gradient
    next_second = BETA_TWO * second + (1.0 - BETA_TWO) * gradient * gradient
    corr_first = next_first / (1.0 - BETA_ONE**STEP_COUNT)
    corr_second = next_second / (1.0 - BETA_TWO**STEP_COUNT)
    updated = weights - rate * (corr_first / (jnp.sqrt(corr_second) + ADAM_EPS) + decay * weights)
    return (updated, next_first, next_second)


def local(
    images,
    cotangent,
    weights_in,
    weights_down,
    vectors,
    mean_in,
    mean_down,
    mean_vectors,
    square_in,
    square_down,
    square_vectors,
):
    halves = (to_half(weights_in), to_half(weights_down), to_half(vectors))
    forward_set = (
        lax.all_gather(halves[0], "shard", axis=0, tiled=True),
        lax.all_gather(halves[1], "shard", axis=0, tiled=True),
        lax.all_gather(halves[2], "shard", axis=1, tiled=True),
    )
    block_out, saved = forward_pass(images, forward_set[0], forward_set[1], forward_set[2])
    backward_set = (
        lax.all_gather(halves[0], "shard", axis=0, tiled=True),
        lax.all_gather(halves[1], "shard", axis=0, tiled=True),
        lax.all_gather(halves[2], "shard", axis=1, tiled=True),
    )
    input_grad, grad_down_local, grad_vectors_local, factors = backward_pass(
        cotangent, saved, backward_set[0], backward_set[1], backward_set[2]
    )
    act_one, grad_proj, attended, hidden_half, act_two, up_half = factors

    def column_part(activation, gradient):
        return transposed_times(activation, gradient)

    owned_in = lax.psum_scatter(
        jnp.concatenate(
            [
                column_part(act_one, grad_proj),
                column_part(attended, hidden_half),
                column_part(act_two, up_half),
            ],
            axis=1,
        ).astype(jnp.bfloat16),
        "shard",
        scatter_dimension=0,
        tiled=True,
    )
    owned_down, owned_vectors = (
        lax.psum_scatter(
            grad_down_local.astype(jnp.bfloat16), "shard", scatter_dimension=0, tiled=True
        ).astype(jnp.float32),
        lax.psum_scatter(
            grad_vectors_local.astype(jnp.bfloat16), "shard", scatter_dimension=1, tiled=True
        ).astype(jnp.float32),
    )
    grad_in, grad_down, grad_vectors = (
        lax.psum(owned_in, "rep").astype(jnp.float32),
        lax.psum(owned_down.astype(jnp.bfloat16), "rep").astype(jnp.float32),
        lax.psum(owned_vectors.astype(jnp.bfloat16), "rep").astype(jnp.float32),
    )
    new_in = adam_update(weights_in, mean_in, square_in, grad_in, RATE_MATRIX, DECAY_MATRIX)
    new_down = adam_update(
        weights_down, mean_down, square_down, grad_down, RATE_MATRIX, DECAY_MATRIX
    )
    new_vectors = adam_update(vectors, mean_vectors, square_vectors, grad_vectors, RATE_VECTOR, 0.0)
    return (
        block_out,
        input_grad,
        grad_in,
        grad_down,
        grad_vectors,
        new_in[0],
        new_down[0],
        new_vectors[0],
        new_in[1],
        new_down[1],
        new_vectors[1],
        new_in[2],
        new_down[2],
        new_vectors[2],
    )


def solution(mesh):
    placed = (
        P(("shard", "rep"), None, None),
        P(("shard", "rep"), None, None),
        P("shard", None),
        P("shard", None),
        P(None, "shard"),
        P("shard", None),
        P("shard", None),
        P(None, "shard"),
        P("shard", None),
        P("shard", None),
        P(None, "shard"),
    )
    return jax.shard_map(
        local,
        mesh=mesh,
        in_specs=placed,
        out_specs=(
            P(("shard", "rep"), None, None),
            P(("shard", "rep"), None, None),
            P("shard", None),
            P("shard", None),
            P(None, "shard"),
            P("shard", None),
            P("shard", None),
            P(None, "shard"),
            P("shard", None),
            P("shard", None),
            P(None, "shard"),
            P("shard", None),
            P("shard", None),
            P(None, "shard"),
        ),
        check_vma=False,
    )
```

profile of v0, /device:TPU:0, one launch (start us, length us, event | category | flops | bytes accessed | tf_op | source)
XLA Modules:
  0.0 623.4 jit_solution(6696602671923517766)
XLA Ops:
  7.2 2.9 convert_element_type.95
  11.2 33.3 %all-gather = bf16[8,96,12]{1,2,0:T(8,128)(2,1)S(1)} all-gather(bf16[1,96,12]{1,2,0:T(8,128)(2,1)S(1)} %convert_bitcast_fusion.1), channel_id=1, replica_groups=mesh['shard'=8,'rep'=4] {'shard'}, dimensions={0}, use_global_device_ids=true | all-gather | bytes 20736 | tf_op jit(solution)/shard_map/all_gather | solution.py:223
  45.1 105.8 %all-gather.4.cloned.1.call-done = bf16[768,6144]{1,0:T(8,128)(2,1)} async-done(((bf16[96,6144]{1,0:T(8,128)(2,1)}), bf16[768,6144]{1,0:T(8,128)(2,1)}) %all-gather.4.cloned.1.call-update) | async-done | bytes 9437200 | tf_op jit(solution)/shard_map/all_gather | solution.py:221
  150.9 3.0 fusion.10
  155.3 1.5 multiply_reduce_fusion.1
  158.0 2.0 fusion.87
  160.3 5.4 multiply_convert_fusion.1
  166.7 3.7 convolution_convert_fusion
  170.7 60.5 %all-gather.6.cloned.1.call-done = bf16[3072,768]{1,0:T(8,128)(2,1)} async-done(((bf16[384,768]{1,0:T(8,128)(2,1)}), bf16[3072,768]{1,0:T(8,128)(2,1)}) %all-gather.6.cloned.1.call-update) | async-done | bytes 4718608 | tf_op jit(solution)/shard_map/all_gather | solution.py:222
  231.2 5.0 fusion.90
  236.2 4.7 multiply_reduce_fusion.2
  240.9 1.4 fusion.84
  242.3 2.5 convolution_convert_fusion.5
  244.8 1.9 copy.66
  246.7 2.5 convolution_convert_fusion.3
  249.2 2.4 copy.70
  251.6 3.0 fusion.91
  254.6 4.7 fusion.30
  259.3 4.9 fusion.86
  265.6 1.3 convolution_convert_fusion.2
  267.1 1.6 convolution_convert_fusion.1
  268.7 4.2 pad_maximum_fusion
  274.3 3.6 fusion.56
  278.9 50.0 %reduce-scatter.8.cloned.1.call-done = bf16[384,768]{1,0:T(8,128)(2,1)} async-done(((bf16[3072,768]{1,0:T(8,128)(2,1)}), bf16[384,768]{1,0:T(8,128)(2,1)}) %reduce-scatter.8.cloned.1.call-update) | async-done | bytes 589840 | tf_op jit(solution)/shard_map/reduce_scatter | solution.py:253
  328.9 165.2 %reduce-scatter.6.cloned.1.call-done = bf16[96,6144]{1,0:T(8,128)(2,1)} async-done(((bf16[768,6144]{1,0:T(8,128)(2,1)}), bf16[96,6144]{1,0:T(8,128)(2,1)}) %reduce-scatter.6.cloned.1.call-update) | async-done | bytes 1179664 | tf_op jit(solution)/shard_map/reduce_scatter | solution.py:239
  494.4 1.4 copy.71
  495.9 4.3 fusion.37
  500.2 58.6 %reduce-scatter.10.cloned.1.call-done = bf16[96,12]{1,0:T(8,128)(2,1)} async-done(((bf16[768,12]{1,0:T(8,128)(2,1)}), bf16[96,12]{1,0:T(8,128)(2,1)}) %reduce-scatter.10.cloned.1.call-update) | async-done | bytes 2320
  559.6 5.7 psum.23
  565.9 40.4 %all-reduce.3.cloned.1.call-done = (bf16[96,6144]{1,0:T(8,128)(2,1)}, bf16[384,768]{1,0:T(8,128)(2,1)}) async-done(((bf16[96,6144]{1,0:T(8,128)(2,1)}, bf16[384,768]{1,0:T(8,128)(2,1)}), (bf16[96,6144]{1,0:T(8,128)(2,1)}, bf16[384,768]{1,0:T(8,128)(2,1)})) %all-reduce.3.cloned.1.call-update) | async-done | bytes 1769488 | tf_op jit(solution)/shard_map/psum | solution.py:261
  606.3 4.6 multiply_subtract_fusion.1
  612.3 4.3 multiply_subtract_fusion
  (118 shorter events, 12.6 us)
Async XLA Ops:
  7.2 3.0 copy-start.3
  7.2 143.7 %all-gather.4.cloned.1.call-start = ((), (), s32[]{:S(2)}) async-start(), calls=%async_computation.3 | async-start | bytes 10616832 | tf_op jit(solution)/shard_map/all_gather | solution.py:221
  10.1 34.5 %copy-start.9 = (bf16[1,197,768]{2,1,0:T(8,128)(2,1)S(1)}, bf16[1,197,768]{2,1,0:T(8,128)(2,1)}, u32[]{:S(2)}) copy-start(bf16[1,197,768]{2,1,0:T(8,128)(2,1)} %param.11) | copy-start | bytes 907780
  10.2 221.0 %all-gather.6.cloned.1.call-start = ((), (), s32[]{:S(2)}) async-start(), calls=%async_computation.4 | async-start | bytes 5308416 | tf_op jit(solution)/shard_map/all_gather | solution.py:222
  11.1 317.8 %reduce-scatter.8.cloned.1.call-start = ((), (), s32[]{:S(2)}) async-start(), calls=%async_computation.6 | async-start | bytes 5308416 | tf_op jit(solution)/shard_map/reduce_scatter | solution.py:253
  155.1 2.2 copy-start.18
  158.0 2.3 copy-start.19
  160.0 76.2 %copy-start.1 = (f32[197,768]{1,0:T(8,128)}, f32[197,768]{1,0:T(8,128)S(1)}, u32[]{:S(2)}) copy-start(f32[197,768]{1,0:T(8,128)S(1)} %get-tuple-element.111) | copy-start | bytes 1815556
  160.3 6.4 %copy-start.13 = (bf16[1,197,768]{2,1,0:T(8,128)(2,1)S(1)}, bf16[1,197,768]{2,1,0:T(8,128)(2,1)}, u32[]{:S(2)}) copy-start(bf16[1,197,768]{2,1,0:T(8,128)(2,1)} %param.12) | copy-start | bytes 907780
  170.4 323.7 %reduce-scatter.6.cloned.1.call-start = ((), (), s32[]{:S(2)}) async-start(), calls=%async_computation.5 | async-start | bytes 10616832 | tf_op jit(solution)/shard_map/reduce_scatter | solution.py:239
  236.2 4.7 copy-start.20
  236.2 4.7 copy-start.14
  259.3 4.9 copy-start.6
  264.1 1.5 copy-start.11
  264.1 1.5 copy-start.28
  264.1 1.5 copy-start.30
  265.6 1.3 copy-start.2
  265.6 1.5 copy-start.21
  267.1 1.6 copy-start.5
  272.9 1.3 copy-start.24
  272.9 1.3 copy-start.29
  272.9 1.4 copy-start.31
  272.9 285.9 %reduce-scatter.10.cloned.1.call-start = ((), (), s32[]{:S(2)}) async-start(), calls=%async_computation.7 | async-start | bytes 221184
  278.9 327.5 %all-reduce.3.cloned.1.call-start = ((), (), s32[]{:S(2)}) async-start(), calls=%async_computation.8 | async-start | bytes 3538944 | tf_op jit(solution)/shard_map/psum | solution.py:261
  494.2 1.7 copy-start.8
  495.9 69.4 %copy-start.26 = (f32[12,96]{1,0:T(8,128)S(1)}, f32[12,96]{1,0:T(8,128)}, u32[]{:S(2)}) copy-start(f32[12,96]{1,0:T(8,128)} %param.18) | copy-start | bytes 13828
  495.9 69.4 %copy-start.27 = (f32[12,96]{1,0:T(8,128)S(1)}, f32[12,96]{1,0:T(8,128)}, u32[]{:S(2)}) copy-start(f32[12,96]{1,0:T(8,128)} %param.21) | copy-start | bytes 13828
  495.9 110.4 %copy-start.4 = (f32[384,768]{1,0:T(8,128)S(1)}, f32[384,768]{1,0:T(8,128)}, u32[]{:S(2)}) copy-start(f32[384,768]{1,0:T(8,128)} %param.14) | copy-start | bytes 3538948
  606.3 4.6 copy-start
  606.3 4.6 copy-start.16
  606.3 5.7 copy-start.17
  606.3 5.9 copy-start.22
  (6 other events, 6.2 us)
Sparse Core Ops, SparseCore 0:
  10.8 140.0 all-gather.3
  153.6 77.5 all-gather.5
  234.9 94.0 reduce-scatter.7
  332.3 161.7 reduce-scatter.5
  497.8 60.9 reduce-scatter.9
  561.2 45.0 all-reduce.2
where the time goes:
time: 624 us; the launch traced here: 623 us
  waiting for transfers between devices  481 us (77%)
  matrix products  54.9 us (9%)
  blocking collectives  38.9 us (6%)
  other arithmetic  20.4 us (3%)
  between operations  14.6 us (2%)
  local copies, waits for them, and re-layouts  13.3 us (2%)
    reduce_scatter x1, waiting for transfers between devices, local(): lax.psum_scatter(jnp.concatenate([column_part(act_one, grad_proj), column...  165 us
    all_gather x1, waiting for transfers between devices, local(): lax.all_gather(halves[0], 'shard', axis=0, tiled=True)  106 us
    all_gather x1, waiting for transfers between devices, local(): lax.all_gather(halves[1], 'shard', axis=0, tiled=True)  60.5 us
    unnamed x7, waiting for transfers between devices  58.7 us
    reduce_scatter x1, waiting for transfers between devices, local(): lax.psum_scatter(grad_down_local.astype(jnp.bfloat16), 'shard', scatter_d...  50 us
    psum x1, waiting for transfers between devices, local(): lax.psum(owned_in, 'rep').astype(jnp.float32)  40.4 us
    all_gather x1, blocking collectives, local(): lax.all_gather(halves[2], 'shard', axis=1, tiled=True)  33.3 us
    dot_general x4, matrix products, times_transposed(): lax.dot_general(left, right, (((1,), (1,)), ((), ())), preferred_element_...  15.7 us
  transfers between devices with their start and end apart: 6, of which 6 were waited for; matrix products, arithmetic and copies ran while one was open for 12% of the time, Pallas kernels for 0%

commit v1 on v0

--- a/solution.py
+++ b/solution.py
@@ -13,6 +13,27 @@
 RATE_VECTOR = 0.15
 DECAY_MATRIX = 0.05
 STEP_COUNT = 2.0
+
+
+def collect(value, axis, dim):
+    size, index, rows = (lax.axis_size(axis), lax.axis_index(axis), value.shape[dim])
+    right = [(i, (i + 1) % size) for i in range(size)]
+    left = [(i, (i - 1) % size) for i in range(size)]
+    result = jnp.zeros((*value.shape[:dim], size * rows, *value.shape[dim + 1 :]), value.dtype)
+    result = lax.dynamic_update_slice_in_dim(result, value, index * rows, axis=dim)
+    from_left = from_right = value
+    half = size // 2
+    for hop in range(1, half + 1):
+        from_left = lax.ppermute(from_left, axis, right)
+        result = lax.dynamic_update_slice_in_dim(
+            result, from_left, (index - hop) % size * rows, axis=dim
+        )
+        if hop < size - half:
+            from_right = lax.ppermute(from_right, axis, left)
+            result = lax.dynamic_update_slice_in_dim(
+                result, from_right, (index + hop) % size * rows, axis=dim
+            )
+    return result
 
 
 def to_half(array_in):
@@ -219,7 +240,7 @@
     halves = (to_half(weights_in), to_half(weights_down), to_half(vectors))
     forward_set = (
         lax.all_gather(halves[0], "shard", axis=0, tiled=True),
-        lax.all_gather(halves[1], "shard", axis=0, tiled=True),
+        collect(halves[1], "shard", 0),
         lax.all_gather(halves[2], "shard", axis=1, tiled=True),
     )
     block_out, saved = forward_pass(images, forward_set[0], forward_set[1], forward_set[2])

time: 624 us -> 682 us (1.093)
  waiting for transfers between devices: 481 us -> 510 us
  starting transfers between devices: 0.65 us -> 18.8 us
  local copies, waits for them, and re-layouts: 13.3 us -> 22.8 us
    ppermute x0 -> x7, waiting for transfers between devices: none -> 95.6 us  [the longest x4 95.6 us: collect(): from_left = lax.ppermute(from_left, axis, right)]
    reduce_scatter x1, waiting for transfers between devices: 50 us -> 0.02 us  [local(): lax.psum_scatter(grad_down_local.astype(jnp.bfloat16), 'shard', scatter_d...]
    ppermute x0 -> x7, starting transfers between devices: none -> 18.3 us  [the longest x3 10.1 us: collect(): from_right = lax.ppermute(from_right, axis, left)]
    reduce_scatter x1, waiting for transfers between devices: 165 us -> 152 us  [local(): lax.psum_scatter(jnp.concatenate([column_part(act_one, grad_proj), column...]
    dynamic_update_slice x0 -> x7, local copies, waits for them, and re-layouts: none -> 7.2 us  [the longest x4 4.54 us: collect(): lax.dynamic_update_slice_in_dim(result, from_left, (index - hop) % size *...]
  transfers between devices with their start and end apart: 6 -> 13, of which waited for: 6 -> 9; matrix products, arithmetic and copies ran while one was open for 12% -> 12% of each run, Pallas kernels for 0% -> 0%
where the time goes in v1:
time: 682 us; the launch traced here: 681 us
  waiting for transfers between devices  510 us (75%)
  matrix products  55 us (8%)
  blocking collectives  39.1 us (6%)
  local copies, waits for them, and re-layouts  22.8 us (3%)
  other arithmetic  21 us (3%)
  starting transfers between devices  18.8 us (3%)
  between operations  14.6 us (2%)
    reduce_scatter x1, waiting for transfers between devices, local(): lax.psum_scatter(jnp.concatenate([column_part(act_one, grad_proj), column...  152 us
    all_gather x1, waiting for transfers between devices, local(): lax.all_gather(halves[0], 'shard', axis=0, tiled=True)  102 us
    ppermute x4, waiting for transfers between devices, collect(): from_left = lax.ppermute(from_left, axis, right)  95.6 us
    all_gather x1, waiting for transfers between devices, local(): lax.all_gather(halves[1], 'shard', axis=0, tiled=True)  60.5 us
    unnamed x7, waiting for transfers between devices  58.7 us
    psum x1, waiting for transfers between devices, local(): lax.psum(owned_in, 'rep').astype(jnp.float32)  40.4 us
    all_gather x1, blocking collectives, local(): lax.all_gather(halves[2], 'shard', axis=1, tiled=True)  33.5 us
    dot_general x4, matrix products, times_transposed(): lax.dot_general(left, right, (((1,), (1,)), ((), ())), preferred_element_...  15.7 us
  transfers between devices with their start and end apart: 13, of which 9 were waited for; matrix products, arithmetic and copies ran while one was open for 12% of the time, Pallas kernels for 0%

profile of v1, /device:TPU:0, one launch (start us, length us, event | category | flops | bytes accessed | tf_op | source)
XLA Modules:
  0.0 681.3 jit_solution(11197868036022037570)
XLA Ops:
  7.2 2.8 convert_element_type.95
  14.6 33.5 %all-gather = bf16[8,96,12]{1,2,0:T(8,128)(2,1)S(1)} all-gather(bf16[1,96,12]{1,2,0:T(8,128)(2,1)S(1)} %convert_bitcast_fusion.1), channel_id=1, replica_groups=mesh['shard'=8,'rep'=4] {'shard'}, dimensions={0}, use_global_device_ids=true | all-gather | bytes 20736 | tf_op jit(solution)/shard_map/all_gather | solution.py:244
  48.6 102.4 %all-gather.4.cloned.1.call-done = bf16[768,6144]{1,0:T(8,128)(2,1)} async-done(((bf16[96,6144]{1,0:T(8,128)(2,1)}), bf16[768,6144]{1,0:T(8,128)(2,1)}) %all-gather.4.cloned.1.call-update) | async-done | bytes 9437200 | tf_op jit(solution)/shard_map/all_gather | solution.py:242
  151.0 3.0 fusion.10
  160.5 5.4 multiply_convert_fusion.1
  166.9 3.6 convolution_convert_fusion
  170.8 60.5 %all-gather.6.cloned.1.call-done = bf16[3072,768]{1,0:T(8,128)(2,1)} async-done(((bf16[384,768]{1,0:T(8,128)(2,1)}), bf16[3072,768]{1,0:T(8,128)(2,1)}) %all-gather.6.cloned.1.call-update) | async-done | bytes 4718608 | tf_op jit(solution)/shard_map/all_gather | solution.py:249
  231.3 5.0 fusion.90
  236.3 4.7 multiply_reduce_fusion.2
  242.4 2.5 convolution_convert_fusion.5
  246.8 2.5 convolution_convert_fusion.3
  251.7 3.0 fusion.91
  254.7 4.7 fusion.30
  259.3 4.8 fusion.86
  268.8 4.2 pad_maximum_fusion
  274.8 4.0 collective-permute-start.1
  278.7 26.1 %collective-permute-done = bf16[384,768]{1,0:T(8,128)(2,1)S(1)} collective-permute-done((bf16[384,768]{1,0:T(8,128)(2,1)S(1)}, bf16[384,768]{1,0:T(8,128)(2,1)S(1)}, u32[]{:S(2)}, u32[]{:S(2)}) %collective-permute-start) | collective-permute-done | bytes 589856 | tf_op jit(solution)/shard_map/ppermute | solution.py:27
  304.9 2.5 collective-permute-start.2
  307.4 2.5 collective-permute-start.3
  309.8 26.8 %collective-permute-done.2 = bf16[384,768]{1,0:T(8,128)(2,1)S(1)} collective-permute-done((bf16[384,768]{1,0:T(8,128)(2,1)S(1)}, bf16[384,768]{1,0:T(8,128)(2,1)S(1)}, u32[]{:S(2)}, u32[]{:S(2)}) %collective-permute-start.2) | collective-permute-done | bytes 589856 | tf_op jit(solution)/shard_map/ppermute | solution.py:27
  336.6 2.5 collective-permute-start.4
  339.2 3.7 collective-permute-start.5
  344.9 23.9 %collective-permute-done.4 = bf16[384,768]{1,0:T(8,128)(2,1)S(1)} collective-permute-done((bf16[384,768]{1,0:T(8,128)(2,1)S(1)}, bf16[384,768]{1,0:T(8,128)(2,1)S(1)}, u32[]{:S(2)}, u32[]{:S(2)}) %collective-permute-start.4) | collective-permute-done | bytes 589856 | tf_op jit(solution)/shard_map/ppermute | solution.py:27
  368.8 2.5 collective-permute-start.6
  375.7 18.8 %collective-permute-done.6 = bf16[384,768]{1,0:T(8,128)(2,1)S(1)} collective-permute-done((bf16[384,768]{1,0:T(8,128)(2,1)S(1)}, bf16[384,768]{1,0:T(8,128)(2,1)S(1)}, u32[]{:S(2)}, u32[]{:S(2)}) %collective-permute-start.6) | collective-permute-done | bytes 589856 | tf_op jit(solution)/shard_map/ppermute | solution.py:27
  395.3 3.5 fusion.56
  400.1 152.4 %reduce-scatter.6.cloned.1.call-done = bf16[96,6144]{1,0:T(8,128)(2,1)} async-done(((bf16[768,6144]{1,0:T(8,128)(2,1)}), bf16[96,6144]{1,0:T(8,128)(2,1)}) %reduce-scatter.6.cloned.1.call-update) | async-done | bytes 1179664 | tf_op jit(solution)/shard_map/reduce_scatter | solution.py:260
  554.3 4.4 fusion.37
  558.7 58.6 %reduce-scatter.10.cloned.1.call-done = bf16[96,12]{1,0:T(8,128)(2,1)} async-done(((bf16[768,12]{1,0:T(8,128)(2,1)}), bf16[96,12]{1,0:T(8,128)(2,1)}) %reduce-scatter.10.cloned.1.call-update) | async-done | bytes 2320
  618.1 5.7 psum.23
  624.4 40.4 %all-reduce.3.cloned.1.call-done = (bf16[96,6144]{1,0:T(8,128)(2,1)}, bf16[384,768]{1,0:T(8,128)(2,1)}) async-done(((bf16[96,6144]{1,0:T(8,128)(2,1)}, bf16[384,768]{1,0:T(8,128)(2,1)}), (bf16[96,6144]{1,0:T(8,128)(2,1)}, bf16[384,768]{1,0:T(8,128)(2,1)})) %all-reduce.3.cloned.1.call-update) | async-done | bytes 1769488 | tf_op jit(solution)/shard_map/psum | solution.py:282
  664.8 7.2 %multiply_subtract_fusion = (f32[96,6144]{1,0:T(8,128)}, f32[96,6144]{1,0:T(8,128)}, f32[96,6144]{1,0:T(8,128)}, f32[96,6144]{1,0:T(8,128)}) fusion(f32[96,6144]{1,0:T(8,128)S(1)} %copy-done, f32[96,6144]{1,0:T(8,128)} %param.16, f32[96,6144]{1,0:T(8,128)} %param.19, bf16[96,6144]{1,0:T(8,128)(2,1)} %get-tuple-element.86), kind=kLoop, calls=%fused_computation.29 | loop fusion | flops 9437184 | bytes 17694720 | tf_op jit(solution)/shard_map/sub | solution.py:223
  (148 shorter events, 38.8 us)
Async XLA Ops:
  7.2 143.8 %all-gather.4.cloned.1.call-start = ((), (), s32[]{:S(2)}) async-start(), calls=%async_computation.3 | async-start | bytes 10616832 | tf_op jit(solution)/shard_map/all_gather | solution.py:242
  10.1 221.2 %all-gather.6.cloned.1.call-start = ((), (), s32[]{:S(2)}) async-start(), calls=%async_computation.4 | async-start | bytes 5308416 | tf_op jit(solution)/shard_map/all_gather | solution.py:249
  11.3 36.9 %copy-start.11 = (bf16[1,197,768]{2,1,0:T(8,128)(2,1)S(1)}, bf16[1,197,768]{2,1,0:T(8,128)(2,1)}, u32[]{:S(2)}) copy-start(bf16[1,197,768]{2,1,0:T(8,128)(2,1)} %param.11) | copy-start | bytes 907780
  14.5 385.6 %reduce-scatter.8.cloned.1.call-start = ((), (), s32[]{:S(2)}) async-start(), calls=%async_computation.6 | async-start | bytes 5308416 | tf_op jit(solution)/shard_map/reduce_scatter | solution.py:274
  160.3 76.0 %copy-start.1 = (f32[197,768]{1,0:T(8,128)}, f32[197,768]{1,0:T(8,128)S(1)}, u32[]{:S(2)}) copy-start(f32[197,768]{1,0:T(8,128)S(1)} %get-tuple-element.113) | copy-start | bytes 1815556
  160.5 6.4 copy-start.15
  170.6 381.9 %reduce-scatter.6.cloned.1.call-start = ((), (), s32[]{:S(2)}) async-start(), calls=%async_computation.5 | async-start | bytes 10616832 | tf_op jit(solution)/shard_map/reduce_scatter | solution.py:260
  236.3 4.7 copy-start.21
  236.3 4.7 copy-start.16
  259.3 4.8 copy-start.8
  272.9 66.2 %copy-start.17 = (bf16[1,197,768]{2,1,0:T(8,128)(2,1)S(1)}, bf16[1,197,768]{2,1,0:T(8,128)(2,1)}, u32[]{:S(2)}) copy-start(bf16[1,197,768]{2,1,0:T(8,128)(2,1)} %param.12) | copy-start | bytes 907780
  273.0 344.3 %reduce-scatter.10.cloned.1.call-start = ((), (), s32[]{:S(2)}) async-start(), calls=%async_computation.7 | async-start | bytes 221184
  274.0 30.9 %collective-permute-start = (bf16[384,768]{1,0:T(8,128)(2,1)S(1)}, bf16[384,768]{1,0:T(8,128)(2,1)S(1)}, u32[]{:S(2)}, u32[]{:S(2)}) collective-permute-start(bf16[384,768]{1,0:T(8,128)(2,1)S(1)} %copy-done.18), channel_id=1, source_target_pairs={{0,4},{4,8},{8,12},{12,16},{16,20},{20,24},{24,28},{28,0},{1,5},{5... | collective-permute-start | bytes 1769480 | tf_op jit(solution)/shard_map/ppermute | solution.py:27
  274.8 32.6 %collective-permute-start.1 = (bf16[384,768]{1,0:T(8,128)(2,1)S(1)}, bf16[384,768]{1,0:T(8,128)(2,1)S(1)}, u32[]{:S(2)}, u32[]{:S(2)}) collective-permute-start(bf16[384,768]{1,0:T(8,128)(2,1)S(1)} %copy-done.18), channel_id=1, source_target_pairs={{0,28},{4,0},{8,4},{12,8},{16,12},{20,16},{24,20},{28,24},{1,29},{... | collective-permute-start | bytes 1769480 | tf_op jit(solution)/shard_map/ppermute | solution.py:32
  304.9 31.7 %copy-start.26 = (bf16[384,768]{1,0:T(8,128)(2,1)}, bf16[384,768]{1,0:T(8,128)(2,1)S(1)}, u32[]{:S(2)}) copy-start(bf16[384,768]{1,0:T(8,128)(2,1)S(1)} %collective-permute-done) | copy-start | bytes 1769476
  304.9 31.7 %collective-permute-start.2 = (bf16[384,768]{1,0:T(8,128)(2,1)S(1)}, bf16[384,768]{1,0:T(8,128)(2,1)S(1)}, u32[]{:S(2)}, u32[]{:S(2)}) collective-permute-start(bf16[384,768]{1,0:T(8,128)(2,1)S(1)} %collective-permute-done), channel_id=1, source_target_pairs={{0,4},{4,8},{8,12},{12,16},{16,20},{20,24},{24,28},{28,0},{1,5},{5... | collective-permute-start | bytes 1769480 | tf_op jit(solution)/shard_map/ppermute | solution.py:27
  307.4 31.9 %collective-permute-start.3 = (bf16[384,768]{1,0:T(8,128)(2,1)S(1)}, bf16[384,768]{1,0:T(8,128)(2,1)S(1)}, u32[]{:S(2)}, u32[]{:S(2)}) collective-permute-start(bf16[384,768]{1,0:T(8,128)(2,1)S(1)} %collective-permute-done.1), channel_id=1, source_target_pairs={{0,28},{4,0},{8,4},{12,8},{16,12},{20,16},{24,20},{28,24},{1,29},{... | collective-permute-start | bytes 1769480 | tf_op jit(solution)/shard_map/ppermute | solution.py:32
  336.6 32.2 %collective-permute-start.4 = (bf16[384,768]{1,0:T(8,128)(2,1)S(1)}, bf16[384,768]{1,0:T(8,128)(2,1)S(1)}, u32[]{:S(2)}, u32[]{:S(2)}) collective-permute-start(bf16[384,768]{1,0:T(8,128)(2,1)S(1)} %collective-permute-done.2), channel_id=1, source_target_pairs={{0,4},{4,8},{8,12},{12,16},{16,20},{20,24},{24,28},{28,0},{1,5},{5... | collective-permute-start | bytes 1769480 | tf_op jit(solution)/shard_map/ppermute | solution.py:27
  339.2 35.5 %collective-permute-start.5 = (bf16[384,768]{1,0:T(8,128)(2,1)S(1)}, bf16[384,768]{1,0:T(8,128)(2,1)S(1)}, u32[]{:S(2)}, u32[]{:S(2)}) collective-permute-start(bf16[384,768]{1,0:T(8,128)(2,1)S(1)} %collective-permute-done.3), channel_id=1, source_target_pairs={{0,28},{4,0},{8,4},{12,8},{16,12},{20,16},{24,20},{28,24},{1,29},{... | collective-permute-start | bytes 1769480 | tf_op jit(solution)/shard_map/ppermute | solution.py:32
  368.8 25.7 %collective-permute-start.6 = (bf16[384,768]{1,0:T(8,128)(2,1)S(1)}, bf16[384,768]{1,0:T(8,128)(2,1)S(1)}, u32[]{:S(2)}, u32[]{:S(2)}) collective-permute-start(bf16[384,768]{1,0:T(8,128)(2,1)S(1)} %collective-permute-done.4), channel_id=1, source_target_pairs={{0,4},{4,8},{8,12},{12,16},{16,20},{20,24},{24,28},{28,0},{1,5},{5... | collective-permute-start | bytes 1769480 | tf_op jit(solution)/shard_map/ppermute | solution.py:27
  373.0 22.3 %copy-start.14 = (bf16[1,197,768]{2,1,0:T(8,128)(2,1)S(1)}, bf16[1,197,768]{2,1,0:T(8,128)(2,1)}, u32[]{:S(2)}) copy-start(bf16[1,197,768]{2,1,0:T(8,128)(2,1)} %param.11) | copy-start | bytes 907780
  373.0 22.3 %copy-start.28 = (bf16[1,197,12,64]{1,3,2,0:T(8,128)(2,1)S(1)}, bf16[1,197,12,64]{1,3,2,0:T(8,128)(2,1)}, u32[]{:S(2)}) copy-start(bf16[1,197,12,64]{1,3,2,0:T(8,128)(2,1)} %copy-done.27) | copy-start | bytes 907780
  373.0 22.3 %copy-start.33 = (bf16[12,64,197]{2,1,0:T(8,128)(2,1)S(1)}, bf16[12,64,197]{2,1,0:T(8,128)(2,1)}, u32[]{:S(2)}) copy-start(bf16[12,64,197]{2,1,0:T(8,128)(2,1)} %fusion.30) | copy-start | bytes 907780
  373.0 22.3 %copy-start.35 = (bf16[1,197,12,64]{1,3,2,0:T(8,128)(2,1)S(1)}, bf16[1,197,12,64]{1,3,2,0:T(8,128)(2,1)}, u32[]{:S(2)}) copy-start(bf16[1,197,12,64]{1,3,2,0:T(8,128)(2,1)} %get-tuple-element.109) | copy-start | bytes 907780
  400.0 264.7 %all-reduce.3.cloned.1.call-start = ((), (), s32[]{:S(2)}) async-start(), calls=%async_computation.8 | async-start | bytes 3538944 | tf_op jit(solution)/shard_map/psum | solution.py:282
  554.3 69.5 %copy-start.30 = (f32[12,96]{1,0:T(8,128)S(1)}, f32[12,96]{1,0:T(8,128)}, u32[]{:S(2)}) copy-start(f32[12,96]{1,0:T(8,128)} %param.18) | copy-start | bytes 13828
  554.3 69.5 %copy-start.31 = (f32[12,96]{1,0:T(8,128)S(1)}, f32[12,96]{1,0:T(8,128)}, u32[]{:S(2)}) copy-start(f32[12,96]{1,0:T(8,128)} %param.21) | copy-start | bytes 13828
  554.3 110.5 %copy-start = (f32[96,6144]{1,0:T(8,128)S(1)}, f32[96,6144]{1,0:T(8,128)}, u32[]{:S(2)}) copy-start(f32[96,6144]{1,0:T(8,128)} %param.13) | copy-start | bytes 7077892
  664.8 7.2 %copy-start.5 = (f32[384,768]{1,0:T(8,128)S(1)}, f32[384,768]{1,0:T(8,128)}, u32[]{:S(2)}) copy-start(f32[384,768]{1,0:T(8,128)} %param.14) | copy-start | bytes 3538948
  664.8 7.2 %copy-start.23 = (f32[384,768]{1,0:T(8,128)S(1)}, f32[384,768]{1,0:T(8,128)}, u32[]{:S(2)}) copy-start(f32[384,768]{1,0:T(8,128)} %param.17) | copy-start | bytes 3538948
  664.8 7.2 %copy-start.24 = (f32[384,768]{1,0:T(8,128)S(1)}, f32[384,768]{1,0:T(8,128)}, u32[]{:S(2)}) copy-start(f32[384,768]{1,0:T(8,128)} %param.20) | copy-start | bytes 3538948
  664.8 7.2 %copy-start.25 = (bf16[384,768]{1,0:T(8,128)(2,1)S(1)}, bf16[384,768]{1,0:T(8,128)(2,1)}, u32[]{:S(2)}) copy-start(bf16[384,768]{1,0:T(8,128)(2,1)} %get-tuple-element.87) | copy-start | bytes 1769476
  (17 other events, 27.5 us)
Sparse Core Ops, SparseCore 0:
  10.7 140.2 all-gather.3
  153.8 77.4 all-gather.5
  234.9 142.9 reduce-scatter.7
  381.4 171.0 reduce-scatter.5
  556.2 61.0 reduce-scatter.9
  619.6 45.0 all-reduce.2
